TPU v7x, 32 devices: a whole 2x2x4 slice. The times are simulated.
32 devices in a mesh: batch: 8 (over y, x, core), tensor: 4 (over z).
Axes of the slice: x: 2, y: 2, z: 4, core: 2. Of those that a mesh axis runs over, the one named last changes fastest.
Arguments:
- slot_states: bfloat16 [960, 32, 768], P('tensor', 'batch'), may hold values from -6 to 6
- pass_counts: int32 [32], P('batch'), may hold values from 2 to 5
- w_qkv: bfloat16 [768, 3, 768], P(None, None, 'tensor'), may hold values from -0.21875 to 0.21875
- q_bias: bfloat16 [768], P('tensor'), may hold values from -3 to 3
- v_bias: bfloat16 [768], P('tensor'), may hold values from -0.29882812 to 0.29882812
- w_out: bfloat16 [768, 768], P('tensor'), may hold values from -1.75 to 1.75
- out_bias: bfloat16 [768], replicated, may hold values from -3 to 3
- w_up: bfloat16 [768, 3072], P(None, 'tensor'), may hold values from -0.21875 to 0.21875
- up_bias: bfloat16 [3072], P('tensor'), may hold values from -3 to 3
- w_down: bfloat16 [3072, 768], P('tensor'), may hold values from -0.109375 to 0.109375
- down_bias: bfloat16 [768], replicated, may hold values from -3 to 3
- ln1_gain: bfloat16 [768], replicated, may hold values from 0.099609375 to 1.8984375
- ln1_bias: bfloat16 [768], replicated, may hold values from -2 to 2
- ln2_gain: bfloat16 [768], replicated, may hold values from 0.099609375 to 1.8984375
- ln2_bias: bfloat16 [768], replicated, may hold values from -2 to 2
- pass_table: bfloat16 [5, 768], replicated, may hold values from -5 to 5
- cotangent: bfloat16 [960, 32, 768], P('tensor', 'batch'), may hold values from -6 to 6
Outputs:
- layer_out: bfloat16 [960, 32, 768], P('tensor', 'batch')
- grad_states: bfloat16 [960, 32, 768], P('tensor', 'batch')
- grad_qkv: float32 [768, 3, 768], P(None, None, 'tensor')
- grad_q_bias: float32 [768], P('tensor')
- grad_v_bias: float32 [768], P('tensor')
- grad_out: float32 [768, 768], P('tensor')
- grad_out_bias: float32 [768], replicated
- grad_up: float32 [768, 3072], P(None, 'tensor')
- grad_up_bias: float32 [3072], P('tensor')
- grad_down: float32 [3072, 768], P('tensor')
- grad_down_bias: float32 [768], replicated
- grad_ln1_gain: float32 [768], replicated
- grad_ln1_bias: float32 [768], replicated
- grad_ln2_gain: float32 [768], replicated
- grad_ln2_bias: float32 [768], replicated
- grad_pass: float32 [5, 768], replicated
All inputs are finite; a program needn't handle non-finite values.
Results may differ from a plain program's by a relative error of at most 0.02.
Values may be sent and summed in bfloat16 or wider, within the bound.
No kernel may reach another device: no remote copies, remote signals or barrier semaphores. Data moves between devices by JAX's collectives and lax.ppermute only.
A program may use at most 256 MiB of HBM per device.

v0:
```python
import math
import jax
import jax.numpy as jnp
from jax import lax
from jax.sharding import PartitionSpec as P

HEAD_DIM = 64
PASSES = 5
LEN = 192
MICRO = 4
SEQ_DEV = 1
HIGHEST = lax.Precision.HIGHEST
EPSILON = 1e-05
MASKED = -1e30


def norm_rows(values, gain, shift):
    center = values - jnp.mean(values, axis=-1, keepdims=True)
    spread = jnp.mean(center * center, axis=-1, keepdims=True)
    return center * lax.rsqrt(spread + EPSILON) * gain + shift


def gelu_tanh(values):
    return jax.nn.gelu(values, approximate=True)


def block_scores(query, keys, allowed, scale):
    scores = jnp.einsum("qbhd,kbhd->bhqk", query, keys, preferred_element_type=jnp.float32) * scale
    return jnp.where(allowed, scores, MASKED)


def attend_block(query, keys, values, allowed, scale):
    scores = block_scores(query, keys, allowed, scale)
    peak = jnp.max(scores, axis=-1, keepdims=True)
    powers = jnp.exp(scores - peak)
    total = jnp.sum(powers, axis=-1, keepdims=True)
    weights = (powers / total).astype(jnp.bfloat16)
    mixed = jnp.einsum("bhqk,kbhd->qbhd", weights, values, preferred_element_type=jnp.float32)
    return (mixed.astype(jnp.bfloat16), peak + jnp.log(total))


def attend_back(query, keys, values, allowed, log_total, grad_mixed, scale):
    scores = block_scores(query, keys, allowed, scale)
    probs = jnp.exp(scores - log_total)
    grad_weights = jnp.einsum(
        "qbhd,kbhd->bhqk", grad_mixed, values, preferred_element_type=jnp.float32
    )
    inner = jnp.sum(probs * grad_weights, axis=-1, keepdims=True)
    grad_scores = (probs * (grad_weights - inner)).astype(jnp.bfloat16)
    grad_query = (
        jnp.einsum("bhqk,kbhd->qbhd", grad_scores, keys, preferred_element_type=jnp.float32) * scale
    )
    grad_keys = (
        jnp.einsum("bhqk,qbhd->kbhd", grad_scores, query, preferred_element_type=jnp.float32)
        * scale
    )
    grad_values = jnp.einsum(
        "bhqk,qbhd->kbhd",
        probs.astype(jnp.bfloat16),
        grad_mixed,
        preferred_element_type=jnp.float32,
    )
    return (grad_query, grad_keys, grad_values)


def layer_block(states, counts, cot_rows, row_index, slots, weights, norms, links):
    qkv_matrix, q_bias, v_bias, w_out, bias_output, w_up, bias_upward, w_down, bias_downward = (
        weights
    )
    gain_one, shift_one, gain_two, shift_two, table = norms
    (
        gather_first,
        sum_attn,
        gather_second,
        sum_mlp,
        gather_grad,
        sum_upward,
        gather_attn,
        sum_qkv,
    ) = links
    width = states.shape[2]
    nseq = states.shape[1]
    local_width = qkv_matrix.shape[1] // 3
    heads_here = local_width // HEAD_DIM
    scale = 1.0 / math.sqrt(HEAD_DIM)
    full_index = jnp.arange(slots, dtype=jnp.int32)
    bias_query = q_bias.astype(jnp.float32).reshape(heads_here, HEAD_DIM)
    bias_value = v_bias.astype(jnp.float32).reshape(heads_here, HEAD_DIM)
    passes = row_index[:, None] % counts[None, :]
    onehot = (passes[:, :, None] == jnp.arange(PASSES, dtype=jnp.int32)[None, None, :]).astype(
        jnp.float32
    )
    live_rows = row_index[:, None] < counts[None, :] * LEN
    allowed = (full_index[None, None, :] <= full_index[None, :, None]) & (
        full_index[None, None, :] < (counts * LEN)[:, None, None]
    )
    hidden = states + jnp.einsum("rbp,pd->rbd", onehot, table, precision=HIGHEST)
    norm_one, pull_one = jax.vjp(norm_rows, hidden, gain_one, shift_one)
    gathered_one = gather_first(norm_one.astype(jnp.bfloat16))
    projected = jnp.einsum(
        "sbd,dc->sbc", gathered_one, qkv_matrix, preferred_element_type=jnp.float32
    )
    projected = projected.reshape(slots, nseq, 3, heads_here, HEAD_DIM)
    query = (projected[:, :, 0] + bias_query).astype(jnp.bfloat16)
    keys = projected[:, :, 1].astype(jnp.bfloat16)
    values = (projected[:, :, 2] + bias_value).astype(jnp.bfloat16)
    piece_number = 0
    begin = piece_number * slots
    mixed, log_total = attend_block(
        query, keys, values, allowed[:, None, begin : begin + slots], scale
    )
    log_blocks = [log_total]
    mixed_flat = mixed.reshape(slots, nseq, local_width)

    def attn_term(start, count):
        return jnp.einsum("sbc,cd->sbd", mixed_flat, w_out, preferred_element_type=jnp.float32)

    attn_total = sum_attn(attn_term)
    after = hidden + attn_total + bias_output
    norm_two, pull_two = jax.vjp(norm_rows, after, gain_two, shift_two)
    gathered_two = gather_second(norm_two.astype(jnp.bfloat16))
    pre_act = (
        jnp.einsum("sbd,df->sbf", gathered_two, w_up, preferred_element_type=jnp.float32)
        + bias_upward
    )
    activated, pull_act = jax.vjp(gelu_tanh, pre_act)
    act_low = activated.astype(jnp.bfloat16)

    def mlp_term(start, count):
        return jnp.einsum("sbf,fd->sbd", act_low, w_down, preferred_element_type=jnp.float32)

    mlp_total = sum_mlp(mlp_term)
    result = after + mlp_total + bias_downward
    layer_part = jnp.where(live_rows[:, :, None], result, 0.0).astype(jnp.bfloat16)
    grad_result = jnp.where(live_rows[:, :, None], cot_rows.astype(jnp.float32), 0.0)
    grad_branch = gather_grad(grad_result.astype(jnp.bfloat16))
    grad_down_part = jnp.einsum(
        "sbf,sbd->fd", act_low, grad_branch, preferred_element_type=jnp.float32
    )
    grad_act = jnp.einsum("sbd,fd->sbf", grad_branch, w_down, preferred_element_type=jnp.float32)
    grad_pre = pull_act(grad_act)[0].astype(jnp.bfloat16)
    grad_up_part = jnp.einsum(
        "sbd,sbf->df", gathered_two, grad_pre, preferred_element_type=jnp.float32
    )
    grad_up_bias_part = jnp.sum(grad_pre.astype(jnp.float32), axis=(0, 1))

    def upward_term(start, count):
        return jnp.einsum("sbf,df->sbd", grad_pre, w_up, preferred_element_type=jnp.float32)

    grad_norm_two = sum_upward(upward_term)
    grad_after, grad_gain_two, grad_shift_two = pull_two(grad_norm_two)
    grad_after = grad_after + grad_result
    grad_out_bias_part = jnp.sum(grad_after, axis=(0, 1))
    grad_down_bias_part = jnp.sum(grad_result, axis=(0, 1))
    grad_attn = gather_attn(grad_after.astype(jnp.bfloat16))
    grad_out_part = jnp.einsum(
        "sbc,sbd->cd", mixed_flat, grad_attn, preferred_element_type=jnp.float32
    )
    grad_mixed = jnp.einsum("sbd,cd->sbc", grad_attn, w_out, preferred_element_type=jnp.float32)
    grad_mixed = grad_mixed.astype(jnp.bfloat16).reshape(slots, nseq, heads_here, HEAD_DIM)
    piece_number = 0
    begin = piece_number * slots
    grad_query, grad_keys, grad_values = attend_back(
        query,
        keys,
        values,
        allowed[:, None, begin : begin + slots],
        log_blocks[piece_number],
        grad_mixed,
        scale,
    )
    grad_proj = jnp.stack([grad_query, grad_keys, grad_values], axis=2)
    grad_proj = grad_proj.astype(jnp.bfloat16).reshape(slots, nseq, 3 * local_width)
    grad_qkv_part = jnp.einsum(
        "sbd,sbc->dc", gathered_one, grad_proj, preferred_element_type=jnp.float32
    ).reshape(width, 3, local_width)
    rounded_proj = grad_proj.astype(jnp.float32).reshape(slots, nseq, 3, local_width)
    grad_q_bias_part = jnp.sum(rounded_proj[:, :, 0], axis=(0, 1))
    grad_v_bias_part = jnp.sum(rounded_proj[:, :, 2], axis=(0, 1))

    def qkv_term(start, count):
        return jnp.einsum("sbc,dc->sbd", grad_proj, qkv_matrix, preferred_element_type=jnp.float32)

    grad_norm_one = sum_qkv(qkv_term)
    grad_hidden, grad_gain_one, grad_shift_one = pull_one(grad_norm_one)
    grad_hidden = grad_hidden + grad_after
    grad_part = grad_hidden.astype(jnp.bfloat16)
    grad_pass_part = jnp.einsum("rbp,rbd->pd", onehot, grad_hidden, precision=HIGHEST)
    matrices = (grad_qkv_part, grad_out_part, grad_up_part, grad_down_part)
    shared = (
        grad_gain_one,
        grad_shift_one,
        grad_gain_two,
        grad_shift_two,
        grad_out_bias_part,
        grad_down_bias_part,
        grad_pass_part,
    )
    biases = (grad_q_bias_part, grad_v_bias_part, grad_up_bias_part)
    return (layer_part, grad_part, matrices, shared, biases)


def add_tuples(old, new):
    if old is None:
        return new
    return tuple((first + second for first, second in zip(old, new)))


def per_device(
    slot_states,
    pass_counts,
    w_qkv,
    q_bias,
    v_bias,
    w_out,
    out_bias,
    w_up,
    up_bias,
    w_down,
    down_bias,
    ln1_gain,
    ln1_bias,
    ln2_gain,
    ln2_bias,
    pass_table,
    cotangent,
):
    groups = lax.axis_size("tensor")
    rows = slot_states.shape[0]
    slots = rows * groups
    norms = (
        ln1_gain.astype(jnp.float32),
        ln1_bias.astype(jnp.float32),
        ln2_gain.astype(jnp.float32),
        ln2_bias.astype(jnp.float32),
        pass_table.astype(jnp.float32),
    )
    bias_output = out_bias.astype(jnp.float32)
    bias_downward = down_bias.astype(jnp.float32)
    layer_parts = []
    grad_parts = []
    matrix_totals = None
    shared_totals = None
    bias_totals = None
    width = slot_states.shape[2]
    weights = (
        w_qkv.reshape(width, 3 * w_qkv.shape[2]),
        q_bias,
        v_bias,
        w_out,
        bias_output,
        w_up,
        up_bias.astype(jnp.float32),
        w_down,
        bias_downward,
    )
    row_index = lax.axis_index("tensor") * rows + jnp.arange(rows, dtype=jnp.int32)

    def gather_first(values):
        return lax.all_gather(values, "tensor", axis=0, tiled=True)

    def sum_attn(term):
        return lax.psum_scatter(
            term(jnp.int32(0), lax.axis_size("tensor") * rows).astype(jnp.bfloat16),
            "tensor",
            scatter_dimension=0,
            tiled=True,
        ).astype(jnp.float32)

    def gather_second(values):
        return lax.all_gather(values, "tensor", axis=0, tiled=True)

    def sum_mlp(term):
        return lax.psum_scatter(
            term(jnp.int32(0), lax.axis_size("tensor") * rows).astype(jnp.bfloat16),
            "tensor",
            scatter_dimension=0,
            tiled=True,
        ).astype(jnp.float32)

    def gather_grad(values):
        return lax.all_gather(values, "tensor", axis=0, tiled=True)

    def sum_upward(term):
        return lax.psum_scatter(
            term(jnp.int32(0), lax.axis_size("tensor") * rows).astype(jnp.bfloat16),
            "tensor",
            scatter_dimension=0,
            tiled=True,
        ).astype(jnp.float32)

    def gather_attn(values):
        return lax.all_gather(values, "tensor", axis=0, tiled=True)

    def sum_qkv(term):
        return lax.psum_scatter(
            term(jnp.int32(0), lax.axis_size("tensor") * rows).astype(jnp.bfloat16),
            "tensor",
            scatter_dimension=0,
            tiled=True,
        ).astype(jnp.float32)

    links = (
        gather_first,
        sum_attn,
        gather_second,
        sum_mlp,
        gather_grad,
        sum_upward,
        gather_attn,
        sum_qkv,
    )
    for micro in range(MICRO):
        first_seq = micro * SEQ_DEV
        layer_part, grad_part, matrices, shared, biases = layer_block(
            slot_states[:, first_seq : first_seq + SEQ_DEV].astype(jnp.float32),
            pass_counts[first_seq : first_seq + SEQ_DEV],
            cotangent[:, first_seq : first_seq + SEQ_DEV],
            row_index,
            slots,
            weights,
            norms,
            links,
        )
        layer_parts.append(layer_part)
        grad_parts.append(grad_part)
        matrices = (
            lax.psum_scatter(matrices[0], "batch", scatter_dimension=0, tiled=True),
            lax.psum_scatter(matrices[1], "batch", scatter_dimension=0, tiled=True),
            lax.psum_scatter(matrices[2], "batch", scatter_dimension=0, tiled=True),
            lax.psum_scatter(matrices[3], "batch", scatter_dimension=0, tiled=True),
        )
        matrix_totals = add_tuples(matrix_totals, matrices)
        shared_totals = add_tuples(shared_totals, shared)
        bias_totals = add_tuples(bias_totals, biases)
    layer_out = jnp.concatenate(layer_parts, axis=1)
    grad_states = jnp.concatenate(grad_parts, axis=1)
    whole = (
        lax.all_gather(matrix_totals[0].astype(jnp.bfloat16), "batch", axis=0, tiled=True).astype(
            jnp.float32
        ),
        lax.all_gather(matrix_totals[1].astype(jnp.bfloat16), "batch", axis=0, tiled=True).astype(
            jnp.float32
        ),
        lax.all_gather(matrix_totals[2].astype(jnp.bfloat16), "batch", axis=0, tiled=True).astype(
            jnp.float32
        ),
        lax.all_gather(matrix_totals[3].astype(jnp.bfloat16), "batch", axis=0, tiled=True).astype(
            jnp.float32
        ),
    )
    shared_sum = lax.psum(
        (
            shared_totals[0],
            shared_totals[1],
            shared_totals[2],
            shared_totals[3],
            shared_totals[4],
            shared_totals[5],
            shared_totals[6],
        ),
        ("batch", "tensor"),
    )
    bias_sum = lax.psum((bias_totals[0], bias_totals[1], bias_totals[2]), "batch")
    return (
        layer_out,
        grad_states,
        whole[0],
        bias_sum[0],
        bias_sum[1],
        whole[1],
        shared_sum[4],
        whole[2],
        bias_sum[2],
        whole[3],
        shared_sum[5],
        shared_sum[0],
        shared_sum[1],
        shared_sum[2],
        shared_sum[3],
        shared_sum[6],
    )


def solution(mesh):
    in_specs = (
        P("tensor", "batch", None),
        P("batch"),
        P(None, None, "tensor"),
        P("tensor"),
        P("tensor"),
        P("tensor", None),
        P(),
        P(None, "tensor"),
        P("tensor"),
        P("tensor", None),
        P(),
        P(),
        P(),
        P(),
        P(),
        P(),
        P("tensor", "batch", None),
    )
    out_specs = (
        P("tensor", "batch", None),
        P("tensor", "batch", None),
        P(None, None, "tensor"),
        P("tensor"),
        P("tensor"),
        P("tensor", None),
        P(),
        P(None, "tensor"),
        P("tensor"),
        P("tensor", None),
        P(),
        P(),
        P(),
        P(),
        P(),
        P(),
    )
    return jax.shard_map(
        per_device, mesh=mesh, in_specs=in_specs, out_specs=out_specs, check_vma=False
    )
```

profile of v0, /device:TPU:0, one launch (start us, length us, event | category | flops | bytes accessed | tf_op | source)
XLA Modules:
  0.0 1458.3 jit_solution(311594064871290279)
XLA Ops:
  37.2 29.7 %all-gather.19.cloned.1.call-done = bf16[960,1,768]{2,0,1:T(8,128)(2,1)} async-done(((bf16[240,1,768]{2,0,1:T(8,128)(2,1)}), bf16[960,1,768]{2,0,1:T(8,128)(2,1)}) %all-gather.19.cloned.1.call-update) | async-done | bytes 1474576 | tf_op jit(solution)/shard_map/all_gather | solution.py:260
  82.1 21.3 %all-gather.23.cloned.1.call-done = bf16[960,1,768]{2,0,1:T(8,128)(2,1)} async-done(((bf16[240,1,768]{2,0,1:T(8,128)(2,1)}), bf16[960,1,768]{2,0,1:T(8,128)(2,1)}) %all-gather.23.cloned.1.call-update) | async-done | bytes 1474576 | tf_op jit(solution)/shard_map/all_gather | solution.py:260
  118.2 21.6 %all-gather.27.cloned.1.call-done = bf16[960,1,768]{2,0,1:T(8,128)(2,1)} async-done(((bf16[240,1,768]{2,0,1:T(8,128)(2,1)}), bf16[960,1,768]{2,0,1:T(8,128)(2,1)}) %all-gather.27.cloned.1.call-update) | async-done | bytes 1474576 | tf_op jit(solution)/shard_map/all_gather | solution.py:260
  154.5 21.2 %all-gather.31.cloned.1.call-done = bf16[960,1,768]{2,0,1:T(8,128)(2,1)} async-done(((bf16[240,1,768]{2,0,1:T(8,128)(2,1)}), bf16[960,1,768]{2,0,1:T(8,128)(2,1)}) %all-gather.31.cloned.1.call-update) | async-done | bytes 1474576 | tf_op jit(solution)/shard_map/all_gather | solution.py:260
  189.9 21.3 %reduce-scatter.21.cloned.1.call-done = bf16[240,1,768]{2,0,1:T(8,128)(2,1)} async-done(((bf16[960,1,768]{2,0,1:T(8,128)(2,1)}), bf16[240,1,768]{2,0,1:T(8,128)(2,1)}) %reduce-scatter.21.cloned.1.call-update) | async-done | bytes 368656 | tf_op jit(solution)/shard_map/reduce_scatter | solution.py:263
  211.3 35.5 %reduce-scatter.25.cloned.1.call-done = bf16[240,1,768]{2,0,1:T(8,128)(2,1)} async-done(((bf16[960,1,768]{2,0,1:T(8,128)(2,1)}), bf16[240,1,768]{2,0,1:T(8,128)(2,1)}) %reduce-scatter.25.cloned.1.call-update) | async-done | bytes 368656 | tf_op jit(solution)/shard_map/reduce_scatter | solution.py:263
  246.7 35.6 %reduce-scatter.29.cloned.1.call-done = bf16[240,1,768]{2,0,1:T(8,128)(2,1)} async-done(((bf16[960,1,768]{2,0,1:T(8,128)(2,1)}), bf16[240,1,768]{2,0,1:T(8,128)(2,1)}) %reduce-scatter.29.cloned.1.call-update) | async-done | bytes 368656 | tf_op jit(solution)/shard_map/reduce_scatter | solution.py:263
  282.3 35.0 %reduce-scatter.33.cloned.1.call-done = bf16[240,1,768]{2,0,1:T(8,128)(2,1)} async-done(((bf16[960,1,768]{2,0,1:T(8,128)(2,1)}), bf16[240,1,768]{2,0,1:T(8,128)(2,1)}) %reduce-scatter.33.cloned.1.call-update) | async-done | bytes 368656 | tf_op jit(solution)/shard_map/reduce_scatter | solution.py:263
  361.6 31.1 %all-gather.47.cloned.1.call-done = bf16[960,1,768]{2,0,1:T(8,128)(2,1)} async-done(((bf16[240,1,768]{2,0,1:T(8,128)(2,1)}), bf16[960,1,768]{2,0,1:T(8,128)(2,1)}) %all-gather.47.cloned.1.call-update) | async-done | bytes 1474576 | tf_op jit(solution)/shard_map/all_gather | solution.py:282
  402.4 26.7 %all-gather.29.cloned.1.call-done = bf16[960,1,768]{2,0,1:T(8,128)(2,1)} async-done(((bf16[240,1,768]{2,0,1:T(8,128)(2,1)}), bf16[960,1,768]{2,0,1:T(8,128)(2,1)}) %all-gather.29.cloned.1.call-update) | async-done | bytes 1474576 | tf_op jit(solution)/shard_map/all_gather | solution.py:271
  433.8 31.1 %all-gather.43.cloned.1.call-done = bf16[960,1,768]{2,0,1:T(8,128)(2,1)} async-done(((bf16[240,1,768]{2,0,1:T(8,128)(2,1)}), bf16[960,1,768]{2,0,1:T(8,128)(2,1)}) %all-gather.43.cloned.1.call-update) | async-done | bytes 1474576 | tf_op jit(solution)/shard_map/all_gather | solution.py:282
  479.8 21.0 %all-gather.25.cloned.1.call-done = bf16[960,1,768]{2,0,1:T(8,128)(2,1)} async-done(((bf16[240,1,768]{2,0,1:T(8,128)(2,1)}), bf16[960,1,768]{2,0,1:T(8,128)(2,1)}) %all-gather.25.cloned.1.call-update) | async-done | bytes 1474576 | tf_op jit(solution)/shard_map/all_gather | solution.py:271
  505.4 31.1 %all-gather.39.cloned.1.call-done = bf16[960,1,768]{2,0,1:T(8,128)(2,1)} async-done(((bf16[240,1,768]{2,0,1:T(8,128)(2,1)}), bf16[960,1,768]{2,0,1:T(8,128)(2,1)}) %all-gather.39.cloned.1.call-update) | async-done | bytes 1474576 | tf_op jit(solution)/shard_map/all_gather | solution.py:282
  546.2 26.7 %all-gather.21.cloned.1.call-done = bf16[960,1,768]{2,0,1:T(8,128)(2,1)} async-done(((bf16[240,1,768]{2,0,1:T(8,128)(2,1)}), bf16[960,1,768]{2,0,1:T(8,128)(2,1)}) %all-gather.21.cloned.1.call-update) | async-done | bytes 1474576 | tf_op jit(solution)/shard_map/all_gather | solution.py:271
  577.5 31.1 %all-gather.35.cloned.1.call-done = bf16[960,1,768]{2,0,1:T(8,128)(2,1)} async-done(((bf16[240,1,768]{2,0,1:T(8,128)(2,1)}), bf16[960,1,768]{2,0,1:T(8,128)(2,1)}) %all-gather.35.cloned.1.call-update) | async-done | bytes 1474576 | tf_op jit(solution)/shard_map/all_gather | solution.py:282
  656.9 22.2 %reduce-scatter.45.cloned.1.call-done = bf16[240,1,768]{2,0,1:T(8,128)(2,1)} async-done(((bf16[960,1,768]{2,0,1:T(8,128)(2,1)}), bf16[240,1,768]{2,0,1:T(8,128)(2,1)}) %reduce-scatter.45.cloned.1.call-update) | async-done | bytes 368656 | tf_op jit(solution)/shard_map/reduce_scatter | solution.py:285
  683.7 31.0 %reduce-scatter.31.cloned.1.call-done = bf16[240,1,768]{2,0,1:T(8,128)(2,1)} async-done(((bf16[960,1,768]{2,0,1:T(8,128)(2,1)}), bf16[240,1,768]{2,0,1:T(8,128)(2,1)}) %reduce-scatter.31.cloned.1.call-update) | async-done | bytes 368656 | tf_op jit(solution)/shard_map/reduce_scatter | solution.py:274
  714.7 34.9 %reduce-scatter.41.cloned.1.call-done = bf16[240,1,768]{2,0,1:T(8,128)(2,1)} async-done(((bf16[960,1,768]{2,0,1:T(8,128)(2,1)}), bf16[240,1,768]{2,0,1:T(8,128)(2,1)}) %reduce-scatter.41.cloned.1.call-update) | async-done | bytes 368656 | tf_op jit(solution)/shard_map/reduce_scatter | solution.py:285
  749.6 35.6 %reduce-scatter.37.cloned.1.call-done = bf16[240,1,768]{2,0,1:T(8,128)(2,1)} async-done(((bf16[960,1,768]{2,0,1:T(8,128)(2,1)}), bf16[240,1,768]{2,0,1:T(8,128)(2,1)}) %reduce-scatter.37.cloned.1.call-update) | async-done | bytes 368656 | tf_op jit(solution)/shard_map/reduce_scatter | solution.py:285
  789.2 31.1 %reduce-scatter.35.cloned.1.call-done = bf16[240,1,768]{2,0,1:T(8,128)(2,1)} async-done(((bf16[960,1,768]{2,0,1:T(8,128)(2,1)}), bf16[240,1,768]{2,0,1:T(8,128)(2,1)}) %reduce-scatter.35.cloned.1.call-update) | async-done | bytes 368656 | tf_op jit(solution)/shard_map/reduce_scatter | solution.py:274
  823.7 31.5 %reduce-scatter.23.cloned.1.call-done = bf16[240,1,768]{2,0,1:T(8,128)(2,1)} async-done(((bf16[960,1,768]{2,0,1:T(8,128)(2,1)}), bf16[240,1,768]{2,0,1:T(8,128)(2,1)}) %reduce-scatter.23.cloned.1.call-update) | async-done | bytes 368656 | tf_op jit(solution)/shard_map/reduce_scatter | solution.py:274
  858.9 31.3 %reduce-scatter.27.cloned.1.call-done = bf16[240,1,768]{2,0,1:T(8,128)(2,1)} async-done(((bf16[960,1,768]{2,0,1:T(8,128)(2,1)}), bf16[240,1,768]{2,0,1:T(8,128)(2,1)}) %reduce-scatter.27.cloned.1.call-update) | async-done | bytes 368656 | tf_op jit(solution)/shard_map/reduce_scatter | solution.py:274
  897.5 37.2 %reduce-scatter.57.cloned.1.call-done = f32[96,768]{1,0:T(8,128)} async-done(((f32[768,768]{1,0:T(8,128)}), f32[96,768]{1,0:T(8,128)}) %reduce-scatter.57.cloned.1.call-update) | async-done | bytes 294928 | tf_op jit(solution)/shard_map/reduce_scatter | solution.py:330
  936.6 43.7 %reduce-scatter.59.cloned.1.call-done = f32[96,768]{1,0:T(8,128)} async-done(((f32[768,768]{1,0:T(8,128)}), f32[96,768]{1,0:T(8,128)}) %reduce-scatter.59.cloned.1.call-update) | async-done | bytes 294928 | tf_op jit(solution)/shard_map/reduce_scatter | solution.py:331
  982.2 35.5 %all-gather.41.cloned.1.call-done = bf16[960,1,768]{2,0,1:T(8,128)(2,1)} async-done(((bf16[240,1,768]{2,0,1:T(8,128)(2,1)}), bf16[960,1,768]{2,0,1:T(8,128)(2,1)}) %all-gather.41.cloned.1.call-update) | async-done | bytes 1474576 | tf_op jit(solution)/shard_map/all_gather | solution.py:293
  1206.2 13.7 all-reduce.1
  1236.2 24.4 %reduce-scatter.53.cloned.1.call-done = f32[96,3,192]{2,0,1:T(8,128)} async-done(((f32[768,3,192]{2,0,1:T(8,128)}), f32[96,3,192]{2,0,1:T(8,128)}) %reduce-scatter.53.cloned.1.call-update) | async-done | bytes 221200 | tf_op jit(solution)/shard_map/reduce_scatter | solution.py:328
  1276.2 20.6 %reduce-scatter.51.cloned.1.call-done = bf16[240,1,768]{2,0,1:T(8,128)(2,1)} async-done(((bf16[960,1,768]{2,0,1:T(8,128)(2,1)}), bf16[240,1,768]{2,0,1:T(8,128)(2,1)}) %reduce-scatter.51.cloned.1.call-update) | async-done | bytes 368656 | tf_op jit(solution)/shard_map/reduce_scatter | solution.py:296
  1298.2 33.5 %reduce-scatter.43.cloned.1.call-done = bf16[240,1,768]{2,0,1:T(8,128)(2,1)} async-done(((bf16[960,1,768]{2,0,1:T(8,128)(2,1)}), bf16[240,1,768]{2,0,1:T(8,128)(2,1)}) %reduce-scatter.43.cloned.1.call-update) | async-done | bytes 368656 | tf_op jit(solution)/shard_map/reduce_scatter | solution.py:296
  1331.8 34.9 %reduce-scatter.47.cloned.1.call-done = bf16[240,1,768]{2,0,1:T(8,128)(2,1)} async-done(((bf16[960,1,768]{2,0,1:T(8,128)(2,1)}), bf16[240,1,768]{2,0,1:T(8,128)(2,1)}) %reduce-scatter.47.cloned.1.call-update) | async-done | bytes 368656 | tf_op jit(solution)/shard_map/reduce_scatter | solution.py:296
  1366.6 35.6 %reduce-scatter.39.cloned.1.call-done = bf16[240,1,768]{2,0,1:T(8,128)(2,1)} async-done(((bf16[960,1,768]{2,0,1:T(8,128)(2,1)}), bf16[240,1,768]{2,0,1:T(8,128)(2,1)}) %reduce-scatter.39.cloned.1.call-update) | async-done | bytes 368656 | tf_op jit(solution)/shard_map/reduce_scatter | solution.py:296
  1411.2 40.3 %all-reduce = (f32[768]{0:T(1024)}, f32[768]{0:T(1024)}, f32[768]{0:T(1024)}, f32[768]{0:T(1024)}, f32[768]{0:T(1024)}, /*index=5*/f32[768]{0:T(1024)}, f32[5,768]{1,0:T(8,128)}) all-reduce(f32[768]{0:T(1024)S(1)} %add_add_fusion.33, f32[768]{0:T(1024)S(1)} %add_add_fusion.31, ...), channel_id=1, replica_groups=mesh['batch'=8,'tensor'=4] {'batch','tensor'}, use_global_device_ids=true, to_apply=%region_82.84 | all-reduce | flops 8448 | bytes 67584 | tf_op jit(solution)/shard_map/psum | solution.py:352
  (692 shorter events, 473.5 us)
Async XLA Ops:
  30.2 145.4 %all-gather.31.cloned.1.call-start = ((), (), s32[]{:S(2)}) async-start(), calls=%async_computation.32 | async-start | bytes 1843200 | tf_op jit(solution)/shard_map/all_gather | solution.py:260
  30.8 180.4 %reduce-scatter.21.cloned.1.call-start = ((), (), s32[]{:S(2)}) async-start(), calls=%async_computation.21 | async-start | bytes 1843200 | tf_op jit(solution)/shard_map/reduce_scatter | solution.py:263
  81.6 165.2 %reduce-scatter.25.cloned.1.call-start = ((), (), s32[]{:S(2)}) async-start(), calls=%async_computation.25 | async-start | bytes 1843200 | tf_op jit(solution)/shard_map/reduce_scatter | solution.py:263
  118.0 164.3 %reduce-scatter.29.cloned.1.call-start = ((), (), s32[]{:S(2)}) async-start(), calls=%async_computation.29 | async-start | bytes 1843200 | tf_op jit(solution)/shard_map/reduce_scatter | solution.py:263
  154.2 163.2 %reduce-scatter.33.cloned.1.call-start = ((), (), s32[]{:S(2)}) async-start(), calls=%async_computation.33 | async-start | bytes 1843200 | tf_op jit(solution)/shard_map/reduce_scatter | solution.py:263
  189.8 167.1 %all-gather.33.cloned.1.call-start = ((), (), s32[]{:S(2)}) async-start(), calls=%async_computation.34 | async-start | bytes 1843200 | tf_op jit(solution)/shard_map/all_gather | solution.py:271
  333.3 131.6 %all-gather.43.cloned.1.call-start = ((), (), s32[]{:S(2)}) async-start(), calls=%async_computation.44 | async-start | bytes 1843200 | tf_op jit(solution)/shard_map/all_gather | solution.py:282
  336.7 164.1 %all-gather.25.cloned.1.call-start = ((), (), s32[]{:S(2)}) async-start(), calls=%async_computation.26 | async-start | bytes 1843200 | tf_op jit(solution)/shard_map/all_gather | solution.py:271
  337.4 199.1 %all-gather.39.cloned.1.call-start = ((), (), s32[]{:S(2)}) async-start(), calls=%async_computation.40 | async-start | bytes 1843200 | tf_op jit(solution)/shard_map/all_gather | solution.py:282
  340.8 232.0 %all-gather.21.cloned.1.call-start = ((), (), s32[]{:S(2)}) async-start(), calls=%async_computation.22 | async-start | bytes 1843200 | tf_op jit(solution)/shard_map/all_gather | solution.py:271
  341.4 267.2 %all-gather.35.cloned.1.call-start = ((), (), s32[]{:S(2)}) async-start(), calls=%async_computation.36 | async-start | bytes 1843200 | tf_op jit(solution)/shard_map/all_gather | solution.py:282
  344.7 312.2 %reduce-scatter.49.cloned.1.call-start = ((), (), s32[]{:S(2)}) async-start(), calls=%async_computation.49 | async-start | bytes 1843200 | tf_op jit(solution)/shard_map/reduce_scatter | solution.py:285
  402.3 276.8 %reduce-scatter.45.cloned.1.call-start = ((), (), s32[]{:S(2)}) async-start(), calls=%async_computation.45 | async-start | bytes 1843200 | tf_op jit(solution)/shard_map/reduce_scatter | solution.py:285
  474.5 240.2 %reduce-scatter.31.cloned.1.call-start = ((), (), s32[]{:S(2)}) async-start(), calls=%async_computation.31 | async-start | bytes 1843200 | tf_op jit(solution)/shard_map/reduce_scatter | solution.py:274
  479.5 270.1 %reduce-scatter.41.cloned.1.call-start = ((), (), s32[]{:S(2)}) async-start(), calls=%async_computation.41 | async-start | bytes 1843200 | tf_op jit(solution)/shard_map/reduce_scatter | solution.py:285
  546.1 239.1 %reduce-scatter.37.cloned.1.call-start = ((), (), s32[]{:S(2)}) async-start(), calls=%async_computation.37 | async-start | bytes 1843200 | tf_op jit(solution)/shard_map/reduce_scatter | solution.py:285
  618.2 202.0 %reduce-scatter.35.cloned.1.call-start = ((), (), s32[]{:S(2)}) async-start(), calls=%async_computation.35 | async-start | bytes 1843200 | tf_op jit(solution)/shard_map/reduce_scatter | solution.py:274
  623.2 232.1 %reduce-scatter.23.cloned.1.call-start = ((), (), s32[]{:S(2)}) async-start(), calls=%async_computation.23 | async-start | bytes 1843200 | tf_op jit(solution)/shard_map/reduce_scatter | solution.py:274
  628.3 261.9 %reduce-scatter.27.cloned.1.call-start = ((), (), s32[]{:S(2)}) async-start(), calls=%async_computation.27 | async-start | bytes 1843200 | tf_op jit(solution)/shard_map/reduce_scatter | solution.py:274
  633.6 301.1 %reduce-scatter.57.cloned.1.call-start = ((), (), s32[]{:S(2)}) async-start(), calls=%async_computation.56 | async-start | bytes 2654208 | tf_op jit(solution)/shard_map/reduce_scatter | solution.py:330
  643.9 336.4 %reduce-scatter.59.cloned.1.call-start = ((), (), s32[]{:S(2)}) async-start(), calls=%async_computation.57 | async-start | bytes 2654208 | tf_op jit(solution)/shard_map/reduce_scatter | solution.py:331
  656.9 360.8 %all-gather.41.cloned.1.call-start = ((), (), s32[]{:S(2)}) async-start(), calls=%async_computation.42 | async-start | bytes 1843200 | tf_op jit(solution)/shard_map/all_gather | solution.py:293
  894.9 159.3 %all-gather.49.cloned.1.call-start = ((), (), s32[]{:S(2)}) async-start(), calls=%async_computation.50 | async-start | bytes 1843200 | tf_op jit(solution)/shard_map/all_gather | solution.py:293
  895.7 194.9 %all-gather.45.cloned.1.call-start = ((), (), s32[]{:S(2)}) async-start(), calls=%async_computation.46 | async-start | bytes 1843200 | tf_op jit(solution)/shard_map/all_gather | solution.py:293
  896.6 229.7 %all-gather.37.cloned.1.call-start = ((), (), s32[]{:S(2)}) async-start(), calls=%async_computation.38 | async-start | bytes 1843200 | tf_op jit(solution)/shard_map/all_gather | solution.py:293
  897.4 322.5 %all-gather.51.cloned.1.call-start = ((), (), s32[]{:S(2)}) async-start(), calls=%async_computation.52 | async-start | bytes 1327104 | tf_op jit(solution)/shard_map/all_gather | solution.py:345
  936.4 286.4 %all-gather.53.cloned.1.call-start = ((), (), s32[]{:S(2)}) async-start(), calls=%async_computation.53 | async-start | bytes 1327104 | tf_op jit(solution)/shard_map/all_gather | solution.py:348
  982.0 243.8 %reduce-scatter.55.cloned.1.call-start = ((), (), s32[]{:S(2)}) async-start(), calls=%async_computation.55 | async-start | bytes 663552 | tf_op jit(solution)/shard_map/reduce_scatter | solution.py:329
  1184.9 112.0 %reduce-scatter.51.cloned.1.call-start = ((), (), s32[]{:S(2)}) async-start(), calls=%async_computation.51 | async-start | bytes 1843200 | tf_op jit(solution)/shard_map/reduce_scatter | solution.py:296
  1188.6 143.1 %reduce-scatter.43.cloned.1.call-start = ((), (), s32[]{:S(2)}) async-start(), calls=%async_computation.43 | async-start | bytes 1843200 | tf_op jit(solution)/shard_map/reduce_scatter | solution.py:296
  1192.9 173.8 %reduce-scatter.47.cloned.1.call-start = ((), (), s32[]{:S(2)}) async-start(), calls=%async_computation.47 | async-start | bytes 1843200 | tf_op jit(solution)/shard_map/reduce_scatter | solution.py:296
  1196.6 205.7 %reduce-scatter.39.cloned.1.call-start = ((), (), s32[]{:S(2)}) async-start(), calls=%async_computation.39 | async-start | bytes 1843200 | tf_op jit(solution)/shard_map/reduce_scatter | solution.py:296
  (201 other events, 6011.2 us)
Sparse Core Ops, SparseCore 0:
  28.8 38.0 all-gather.18
  69.1 34.2 all-gather.22
  105.5 34.2 all-gather.26
  141.3 34.2 all-gather.30
  178.4 32.8 reduce-scatter.20
  214.0 32.6 reduce-scatter.24
  284.7 32.6 reduce-scatter.32
  322.8 34.0 all-gather.32
  358.3 34.2 all-gather.46
  394.8 34.2 all-gather.28
  430.6 34.2 all-gather.42
  466.4 34.2 all-gather.24
  502.2 34.2 all-gather.38
  538.5 34.2 all-gather.20
  574.3 34.2 all-gather.34
  610.7 32.8 reduce-scatter.48
  646.4 32.6 reduce-scatter.44
  682.0 32.6 reduce-scatter.30
  716.9 32.6 reduce-scatter.40
  752.5 32.6 reduce-scatter.36
  787.5 32.6 reduce-scatter.34
  893.5 41.1 reduce-scatter.56
  937.9 42.3 reduce-scatter.58
  982.3 35.3 all-gather.40
  1019.8 34.2 all-gather.48
  1056.3 34.2 all-gather.44
  1092.0 34.2 all-gather.36
  1180.5 34.3 reduce-scatter.54
  1218.3 42.2 reduce-scatter.52
  1262.9 33.9 reduce-scatter.50
  1299.0 32.6 reduce-scatter.42
  1333.9 32.6 reduce-scatter.46
  (6 shorter events, 177.2 us)
where the time goes:
time: 1460 us
  waiting for transfers between devices  952 us (65%)
  matrix products  246 us (17%)
  other arithmetic  98.3 us (7%)
  blocking collectives  74.7 us (5%)
  local copies, waits for them, and re-layouts  56.1 us (4%)
  between operations  27.5 us (2%)
    reduce_scatter x4, waiting for transfers between devices, sum_attn(): lax.psum_scatter(term(jnp.int32(0), lax.axis_size('tensor') * rows).astyp...  127 us
    reduce_scatter x4, waiting for transfers between devices, sum_mlp(): lax.psum_scatter(term(jnp.int32(0), lax.axis_size('tensor') * rows).astyp...  125 us
    reduce_scatter x4, waiting for transfers between devices, sum_qkv(): lax.psum_scatter(term(jnp.int32(0), lax.axis_size('tensor') * rows).astyp...  125 us
    all_gather x4, waiting for transfers between devices, gather_grad(): return lax.all_gather(values, 'tensor', axis=0, tiled=True)  124 us
    all_gather x4, waiting for transfers between devices, gather_first(): return lax.all_gather(values, 'tensor', axis=0, tiled=True)  93.8 us
    reduce_scatter x4, waiting for transfers between devices, sum_upward(): lax.psum_scatter(term(jnp.int32(0), lax.axis_size('tensor') * rows).astyp...  92.7 us
    all_gather x4, waiting for transfers between devices, gather_second(): return lax.all_gather(values, 'tensor', axis=0, tiled=True)  86.1 us
    all_gather x4, waiting for transfers between devices, gather_attn(): return lax.all_gather(values, 'tensor', axis=0, tiled=True)  67.8 us
  transfers between devices with their start and end apart: 38, of which 34 were waited for; matrix products, arithmetic and copies ran while one was open for 23% of the time, Pallas kernels for 0%

commit v1 on v0

--- a/solution.py
+++ b/solution.py
@@ -3,6 +3,7 @@
 import jax.numpy as jnp
 from jax import lax
 from jax.sharding import PartitionSpec as P
+from jax.lax import axis_index, axis_size, ppermute
 
 HEAD_DIM = 64
 PASSES = 5
@@ -290,7 +291,22 @@
         ).astype(jnp.float32)
 
     def gather_attn(values):
-        return lax.all_gather(values, "tensor", axis=0, tiled=True)
+
+        def quarters_divide(u):
+            how_many = axis_size("tensor")
+            in_order = tuple(((idx, (idx + 1) % how_many) for idx in range(how_many)))
+            all_rows = tuple(((idx, (idx - 1) % how_many) for idx in range(how_many)))
+            ready, next_value = ([u], [u])
+            for _ in range(how_many // 2):
+                ready.append(ppermute(ready[-1], axis_name="tensor", perm=in_order))
+            at = 0
+            while at < (how_many - 1) // 2:
+                next_value.append(ppermute(next_value[-1], "tensor", perm=all_rows))
+                at += 1
+            u1 = jnp.concatenate([*ready[::-1], *next_value[1:]], 0)
+            return jnp.roll(u1, (axis_index("tensor") - how_many // 2) * u.shape[0], 0)
+
+        return quarters_divide(values)
 
     def sum_qkv(term):
         return lax.psum_scatter(

time: 1460 us -> 1380 us (0.945)
  waiting for transfers between devices: 952 us -> 831 us
  other arithmetic: 98.3 us -> 136 us
  starting transfers between devices: 4.51 us -> 20.6 us
  matrix products: 246 us -> 231 us
    all_gather x4 -> x0, waiting for transfers between devices: 67.8 us -> none  [gather_attn(): return lax.all_gather(values, 'tensor', axis=0, tiled=True)]
    reduce_scatter x1, waiting for transfers between devices: 43.7 us -> 1.6 us  [per_device(): lax.psum_scatter(matrices[3], 'batch', scatter_dimension=0, tiled=True)]
    reduce_scatter x1, waiting for transfers between devices: 37.2 us -> 0.02 us  [per_device(): lax.psum_scatter(matrices[2], 'batch', scatter_dimension=0, tiled=True)]
    another operation x0 -> x4, other arithmetic: none -> 34.9 us
    ppermute x0 -> x12, waiting for transfers between devices: none -> 33.9 us  [the longest x8 33.2 us: quarters_divide(): ready.append(ppermute(ready[-1], axis_name='tensor', perm=in_order))]
    reduce_scatter x4, waiting for transfers between devices: 125 us -> 150 us  [sum_mlp(): lax.psum_scatter(term(jnp.int32(0), lax.axis_size('tensor') * rows).astyp...]
    reduce_scatter x1, waiting for transfers between devices: 24.4 us -> 0.02 us  [per_device(): lax.psum_scatter(matrices[0], 'batch', scatter_dimension=0, tiled=True)]
    ppermute x0 -> x12, starting transfers between devices: none -> 17 us  [the longest x4 9.7 us: quarters_divide(): next_value.append(ppermute(next_value[-1], 'tensor', perm=all_rows))]
  transfers between devices with their start and end apart: 38 -> 46, of which waited for: 34 -> 33; matrix products, arithmetic and copies ran while one was open for 23% -> 26% of each run, Pallas kernels for 0% -> 0%
where the time goes in v1:
time: 1380 us; the launch traced here: 1370 us
  waiting for transfers between devices  831 us (60%)
  matrix products  231 us (17%)
  other arithmetic  136 us (10%)
  blocking collectives  76.9 us (6%)
  local copies, waits for them, and re-layouts  50.4 us (4%)
  between operations  27.9 us (2%)
  starting transfers between devices  20.6 us (1%)
    reduce_scatter x4, waiting for transfers between devices, sum_mlp(): lax.psum_scatter(term(jnp.int32(0), lax.axis_size('tensor') * rows).astyp...  150 us
    reduce_scatter x4, waiting for transfers between devices, sum_attn(): lax.psum_scatter(term(jnp.int32(0), lax.axis_size('tensor') * rows).astyp...  128 us
    all_gather x4, waiting for transfers between devices, gather_grad(): return lax.all_gather(values, 'tensor', axis=0, tiled=True)  125 us
    reduce_scatter x4, waiting for transfers between devices, sum_qkv(): lax.psum_scatter(term(jnp.int32(0), lax.axis_size('tensor') * rows).astyp...  116 us
    all_gather x4, waiting for transfers between devices, gather_first(): return lax.all_gather(values, 'tensor', axis=0, tiled=True)  93.8 us
    reduce_scatter x4, waiting for transfers between devices, sum_upward(): lax.psum_scatter(term(jnp.int32(0), lax.axis_size('tensor') * rows).astyp...  92.8 us
    all_gather x4, waiting for transfers between devices, gather_second(): return lax.all_gather(values, 'tensor', axis=0, tiled=True)  86.5 us
    psum x1, blocking collectives, per_device(): lax.psum((shared_totals[0], shared_totals[1], shared_totals[2], shared_to...  40.3 us
  transfers between devices with their start and end apart: 46, of which 33 were waited for; matrix products, arithmetic and copies ran while one was open for 26% of the time, Pallas kernels for 0%

profile of v1, /device:TPU:0, one launch (start us, length us, event | category | flops | bytes accessed | tf_op | source)
XLA Modules:
  0.0 1374.1 jit_solution(10053224566722302420)
XLA Ops:
  37.1 29.8 %all-gather.15.cloned.1.call-done = bf16[960,1,768]{2,0,1:T(8,128)(2,1)} async-done(((bf16[240,1,768]{2,0,1:T(8,128)(2,1)}), bf16[960,1,768]{2,0,1:T(8,128)(2,1)}) %all-gather.15.cloned.1.call-update) | async-done | bytes 1474576 | tf_op jit(solution)/shard_map/all_gather | solution.py:261
  81.8 21.6 %all-gather.19.cloned.1.call-done = bf16[960,1,768]{2,0,1:T(8,128)(2,1)} async-done(((bf16[240,1,768]{2,0,1:T(8,128)(2,1)}), bf16[960,1,768]{2,0,1:T(8,128)(2,1)}) %all-gather.19.cloned.1.call-update) | async-done | bytes 1474576 | tf_op jit(solution)/shard_map/all_gather | solution.py:261
  118.3 21.6 %all-gather.23.cloned.1.call-done = bf16[960,1,768]{2,0,1:T(8,128)(2,1)} async-done(((bf16[240,1,768]{2,0,1:T(8,128)(2,1)}), bf16[960,1,768]{2,0,1:T(8,128)(2,1)}) %all-gather.23.cloned.1.call-update) | async-done | bytes 1474576 | tf_op jit(solution)/shard_map/all_gather | solution.py:261
  154.7 20.9 %all-gather.27.cloned.1.call-done = bf16[960,1,768]{2,0,1:T(8,128)(2,1)} async-done(((bf16[240,1,768]{2,0,1:T(8,128)(2,1)}), bf16[960,1,768]{2,0,1:T(8,128)(2,1)}) %all-gather.27.cloned.1.call-update) | async-done | bytes 1474576 | tf_op jit(solution)/shard_map/all_gather | solution.py:261
  189.8 21.4 %reduce-scatter.21.cloned.1.call-done = bf16[240,1,768]{2,0,1:T(8,128)(2,1)} async-done(((bf16[960,1,768]{2,0,1:T(8,128)(2,1)}), bf16[240,1,768]{2,0,1:T(8,128)(2,1)}) %reduce-scatter.21.cloned.1.call-update) | async-done | bytes 368656 | tf_op jit(solution)/shard_map/reduce_scatter | solution.py:264
  211.2 35.5 %reduce-scatter.25.cloned.1.call-done = bf16[240,1,768]{2,0,1:T(8,128)(2,1)} async-done(((bf16[960,1,768]{2,0,1:T(8,128)(2,1)}), bf16[240,1,768]{2,0,1:T(8,128)(2,1)}) %reduce-scatter.25.cloned.1.call-update) | async-done | bytes 368656 | tf_op jit(solution)/shard_map/reduce_scatter | solution.py:264
  246.7 35.6 %reduce-scatter.29.cloned.1.call-done = bf16[240,1,768]{2,0,1:T(8,128)(2,1)} async-done(((bf16[960,1,768]{2,0,1:T(8,128)(2,1)}), bf16[240,1,768]{2,0,1:T(8,128)(2,1)}) %reduce-scatter.29.cloned.1.call-update) | async-done | bytes 368656 | tf_op jit(solution)/shard_map/reduce_scatter | solution.py:264
  282.3 35.0 %reduce-scatter.33.cloned.1.call-done = bf16[240,1,768]{2,0,1:T(8,128)(2,1)} async-done(((bf16[960,1,768]{2,0,1:T(8,128)(2,1)}), bf16[240,1,768]{2,0,1:T(8,128)(2,1)}) %reduce-scatter.33.cloned.1.call-update) | async-done | bytes 368656 | tf_op jit(solution)/shard_map/reduce_scatter | solution.py:264
  344.9 12.1 all-gather.29.cloned.1.call-done
  361.6 31.1 %all-gather.37.cloned.1.call-done = bf16[960,1,768]{2,0,1:T(8,128)(2,1)} async-done(((bf16[240,1,768]{2,0,1:T(8,128)(2,1)}), bf16[960,1,768]{2,0,1:T(8,128)(2,1)}) %all-gather.37.cloned.1.call-update) | async-done | bytes 1474576 | tf_op jit(solution)/shard_map/all_gather | solution.py:283
  402.3 26.8 %all-gather.25.cloned.1.call-done = bf16[960,1,768]{2,0,1:T(8,128)(2,1)} async-done(((bf16[240,1,768]{2,0,1:T(8,128)(2,1)}), bf16[960,1,768]{2,0,1:T(8,128)(2,1)}) %all-gather.25.cloned.1.call-update) | async-done | bytes 1474576 | tf_op jit(solution)/shard_map/all_gather | solution.py:272
  433.7 31.2 %all-gather.35.cloned.1.call-done = bf16[960,1,768]{2,0,1:T(8,128)(2,1)} async-done(((bf16[240,1,768]{2,0,1:T(8,128)(2,1)}), bf16[960,1,768]{2,0,1:T(8,128)(2,1)}) %all-gather.35.cloned.1.call-update) | async-done | bytes 1474576 | tf_op jit(solution)/shard_map/all_gather | solution.py:283
  479.8 21.0 %all-gather.21.cloned.1.call-done = bf16[960,1,768]{2,0,1:T(8,128)(2,1)} async-done(((bf16[240,1,768]{2,0,1:T(8,128)(2,1)}), bf16[960,1,768]{2,0,1:T(8,128)(2,1)}) %all-gather.21.cloned.1.call-update) | async-done | bytes 1474576 | tf_op jit(solution)/shard_map/all_gather | solution.py:272
  505.3 31.2 %all-gather.33.cloned.1.call-done = bf16[960,1,768]{2,0,1:T(8,128)(2,1)} async-done(((bf16[240,1,768]{2,0,1:T(8,128)(2,1)}), bf16[960,1,768]{2,0,1:T(8,128)(2,1)}) %all-gather.33.cloned.1.call-update) | async-done | bytes 1474576 | tf_op jit(solution)/shard_map/all_gather | solution.py:283
  546.2 26.6 %all-gather.17.cloned.1.call-done = bf16[960,1,768]{2,0,1:T(8,128)(2,1)} async-done(((bf16[240,1,768]{2,0,1:T(8,128)(2,1)}), bf16[960,1,768]{2,0,1:T(8,128)(2,1)}) %all-gather.17.cloned.1.call-update) | async-done | bytes 1474576 | tf_op jit(solution)/shard_map/all_gather | solution.py:272
  577.5 31.1 %all-gather.31.cloned.1.call-done = bf16[960,1,768]{2,0,1:T(8,128)(2,1)} async-done(((bf16[240,1,768]{2,0,1:T(8,128)(2,1)}), bf16[960,1,768]{2,0,1:T(8,128)(2,1)}) %all-gather.31.cloned.1.call-update) | async-done | bytes 1474576 | tf_op jit(solution)/shard_map/all_gather | solution.py:283
  656.8 22.2 %reduce-scatter.45.cloned.1.call-done = bf16[240,1,768]{2,0,1:T(8,128)(2,1)} async-done(((bf16[960,1,768]{2,0,1:T(8,128)(2,1)}), bf16[240,1,768]{2,0,1:T(8,128)(2,1)}) %reduce-scatter.45.cloned.1.call-update) | async-done | bytes 368656 | tf_op jit(solution)/shard_map/reduce_scatter | solution.py:286
  682.6 32.1 %reduce-scatter.31.cloned.1.call-done = bf16[240,1,768]{2,0,1:T(8,128)(2,1)} async-done(((bf16[960,1,768]{2,0,1:T(8,128)(2,1)}), bf16[240,1,768]{2,0,1:T(8,128)(2,1)}) %reduce-scatter.31.cloned.1.call-update) | async-done | bytes 368656 | tf_op jit(solution)/shard_map/reduce_scatter | solution.py:275
  714.7 34.9 %reduce-scatter.41.cloned.1.call-done = bf16[240,1,768]{2,0,1:T(8,128)(2,1)} async-done(((bf16[960,1,768]{2,0,1:T(8,128)(2,1)}), bf16[240,1,768]{2,0,1:T(8,128)(2,1)}) %reduce-scatter.41.cloned.1.call-update) | async-done | bytes 368656 | tf_op jit(solution)/shard_map/reduce_scatter | solution.py:286
  749.6 35.6 %reduce-scatter.37.cloned.1.call-done = bf16[240,1,768]{2,0,1:T(8,128)(2,1)} async-done(((bf16[960,1,768]{2,0,1:T(8,128)(2,1)}), bf16[240,1,768]{2,0,1:T(8,128)(2,1)}) %reduce-scatter.37.cloned.1.call-update) | async-done | bytes 368656 | tf_op jit(solution)/shard_map/reduce_scatter | solution.py:286
  791.9 40.8 %reduce-scatter.35.cloned.1.call-done = bf16[240,1,768]{2,0,1:T(8,128)(2,1)} async-done(((bf16[960,1,768]{2,0,1:T(8,128)(2,1)}), bf16[240,1,768]{2,0,1:T(8,128)(2,1)}) %reduce-scatter.35.cloned.1.call-update) | async-done | bytes 368656 | tf_op jit(solution)/shard_map/reduce_scatter | solution.py:275
  840.2 40.8 %reduce-scatter.23.cloned.1.call-done = bf16[240,1,768]{2,0,1:T(8,128)(2,1)} async-done(((bf16[960,1,768]{2,0,1:T(8,128)(2,1)}), bf16[240,1,768]{2,0,1:T(8,128)(2,1)}) %reduce-scatter.23.cloned.1.call-update) | async-done | bytes 368656 | tf_op jit(solution)/shard_map/reduce_scatter | solution.py:275
  885.4 36.6 %reduce-scatter.27.cloned.1.call-done = bf16[240,1,768]{2,0,1:T(8,128)(2,1)} async-done(((bf16[960,1,768]{2,0,1:T(8,128)(2,1)}), bf16[240,1,768]{2,0,1:T(8,128)(2,1)}) %reduce-scatter.27.cloned.1.call-update) | async-done | bytes 368656 | tf_op jit(solution)/shard_map/reduce_scatter | solution.py:275
  968.5 15.0 %collective-permute-done.4 = bf16[240,1,768]{2,0,1:T(8,128)(2,1)S(1)} collective-permute-done((bf16[240,1,768]{2,0,1:T(8,128)(2,1)S(1)}, bf16[240,1,768]{2,0,1:T(8,128)(2,1)S(1)}, u32[]{:S(2)}, u32[]{:S(2)}) %collective-permute-start.4) | collective-permute-done | bytes 368672 | tf_op jit(solution)/shard_map/ppermute | solution.py:301
  995.2 11.2 fusion.84
  1153.1 14.1 %all-reduce.1 = (f32[192]{0:T(256)}, f32[192]{0:T(256)}, f32[768]{0:T(1024)}) all-reduce(f32[192]{0:T(256)S(1)} %add_add_fusion.35, f32[192]{0:T(256)S(1)} %add_add_fusion.34, f32[768]{0:T(1024)S(1)} %add_add_fusion.32), channel_id=1, replica_groups=mesh['batch'=8,'tensor'=4] {'batch'}, use_global_device_ids=true, to_apply=%region_68.71 | all-reduce | flops 1152 | bytes 9216 | tf_op jit(solution)/shard_map/psum | solution.py:380
  1185.7 12.7 all_gather.60
  1200.9 11.4 reduce-scatter.51.cloned.1.call-done
  1213.6 33.7 %reduce-scatter.47.cloned.1.call-done = bf16[240,1,768]{2,0,1:T(8,128)(2,1)} async-done(((bf16[960,1,768]{2,0,1:T(8,128)(2,1)}), bf16[240,1,768]{2,0,1:T(8,128)(2,1)}) %reduce-scatter.47.cloned.1.call-update) | async-done | bytes 368656 | tf_op jit(solution)/shard_map/reduce_scatter | solution.py:312
  1247.3 34.9 %reduce-scatter.43.cloned.1.call-done = bf16[240,1,768]{2,0,1:T(8,128)(2,1)} async-done(((bf16[960,1,768]{2,0,1:T(8,128)(2,1)}), bf16[240,1,768]{2,0,1:T(8,128)(2,1)}) %reduce-scatter.43.cloned.1.call-update) | async-done | bytes 368656 | tf_op jit(solution)/shard_map/reduce_scatter | solution.py:312
  1282.2 35.6 %reduce-scatter.39.cloned.1.call-done = bf16[240,1,768]{2,0,1:T(8,128)(2,1)} async-done(((bf16[960,1,768]{2,0,1:T(8,128)(2,1)}), bf16[240,1,768]{2,0,1:T(8,128)(2,1)}) %reduce-scatter.39.cloned.1.call-update) | async-done | bytes 368656 | tf_op jit(solution)/shard_map/reduce_scatter | solution.py:312
  1326.8 40.3 %all-reduce = (f32[768]{0:T(1024)}, f32[768]{0:T(1024)}, f32[768]{0:T(1024)}, f32[768]{0:T(1024)}, f32[768]{0:T(1024)}, /*index=5*/f32[768]{0:T(1024)}, f32[5,768]{1,0:T(8,128)}) all-reduce(f32[768]{0:T(1024)S(1)} %add_add_fusion.33, f32[768]{0:T(1024)S(1)} %add_add_fusion.31, ...), channel_id=1, replica_groups=mesh['batch'=8,'tensor'=4] {'batch','tensor'}, use_global_device_ids=true, to_apply=%region_82.85 | all-reduce | flops 8448 | bytes 67584 | tf_op jit(solution)/shard_map/psum | solution.py:368
  (672 shorter events, 462.1 us)
Async XLA Ops:
  29.4 110.4 %all-gather.23.cloned.1.call-start = ((), (), s32[]{:S(2)}) async-start(), calls=%async_computation.28 | async-start | bytes 1843200 | tf_op jit(solution)/shard_map/all_gather | solution.py:261
  30.2 145.4 %all-gather.27.cloned.1.call-start = ((), (), s32[]{:S(2)}) async-start(), calls=%async_computation.32 | async-start | bytes 1843200 | tf_op jit(solution)/shard_map/all_gather | solution.py:261
  30.8 180.5 %reduce-scatter.21.cloned.1.call-start = ((), (), s32[]{:S(2)}) async-start(), calls=%async_computation.21 | async-start | bytes 1843200 | tf_op jit(solution)/shard_map/reduce_scatter | solution.py:264
  81.5 165.2 %reduce-scatter.25.cloned.1.call-start = ((), (), s32[]{:S(2)}) async-start(), calls=%async_computation.25 | async-start | bytes 1843200 | tf_op jit(solution)/shard_map/reduce_scatter | solution.py:264
  118.0 164.3 %reduce-scatter.29.cloned.1.call-start = ((), (), s32[]{:S(2)}) async-start(), calls=%async_computation.29 | async-start | bytes 1843200 | tf_op jit(solution)/shard_map/reduce_scatter | solution.py:264
  154.2 163.1 %reduce-scatter.33.cloned.1.call-start = ((), (), s32[]{:S(2)}) async-start(), calls=%async_computation.33 | async-start | bytes 1843200 | tf_op jit(solution)/shard_map/reduce_scatter | solution.py:264
  189.7 167.2 %all-gather.29.cloned.1.call-start = ((), (), s32[]{:S(2)}) async-start(), calls=%async_computation.34 | async-start | bytes 1843200 | tf_op jit(solution)/shard_map/all_gather | solution.py:272
  332.6 96.6 %all-gather.25.cloned.1.call-start = ((), (), s32[]{:S(2)}) async-start(), calls=%async_computation.30 | async-start | bytes 1843200 | tf_op jit(solution)/shard_map/all_gather | solution.py:272
  333.3 131.6 %all-gather.35.cloned.1.call-start = ((), (), s32[]{:S(2)}) async-start(), calls=%async_computation.42 | async-start | bytes 1843200 | tf_op jit(solution)/shard_map/all_gather | solution.py:283
  336.6 164.1 %all-gather.21.cloned.1.call-start = ((), (), s32[]{:S(2)}) async-start(), calls=%async_computation.26 | async-start | bytes 1843200 | tf_op jit(solution)/shard_map/all_gather | solution.py:272
  337.4 199.1 %all-gather.33.cloned.1.call-start = ((), (), s32[]{:S(2)}) async-start(), calls=%async_computation.39 | async-start | bytes 1843200 | tf_op jit(solution)/shard_map/all_gather | solution.py:283
  340.7 232.1 %all-gather.17.cloned.1.call-start = ((), (), s32[]{:S(2)}) async-start(), calls=%async_computation.22 | async-start | bytes 1843200 | tf_op jit(solution)/shard_map/all_gather | solution.py:272
  341.3 267.2 %all-gather.31.cloned.1.call-start = ((), (), s32[]{:S(2)}) async-start(), calls=%async_computation.36 | async-start | bytes 1843200 | tf_op jit(solution)/shard_map/all_gather | solution.py:283
  344.7 312.2 %reduce-scatter.49.cloned.1.call-start = ((), (), s32[]{:S(2)}) async-start(), calls=%async_computation.46 | async-start | bytes 1843200 | tf_op jit(solution)/shard_map/reduce_scatter | solution.py:286
  402.3 276.8 %reduce-scatter.45.cloned.1.call-start = ((), (), s32[]{:S(2)}) async-start(), calls=%async_computation.43 | async-start | bytes 1843200 | tf_op jit(solution)/shard_map/reduce_scatter | solution.py:286
  474.5 240.2 %reduce-scatter.31.cloned.1.call-start = ((), (), s32[]{:S(2)}) async-start(), calls=%async_computation.31 | async-start | bytes 1843200 | tf_op jit(solution)/shard_map/reduce_scatter | solution.py:275
  479.5 270.1 %reduce-scatter.41.cloned.1.call-start = ((), (), s32[]{:S(2)}) async-start(), calls=%async_computation.40 | async-start | bytes 1843200 | tf_op jit(solution)/shard_map/reduce_scatter | solution.py:286
  546.1 239.1 %reduce-scatter.37.cloned.1.call-start = ((), (), s32[]{:S(2)}) async-start(), calls=%async_computation.37 | async-start | bytes 1843200 | tf_op jit(solution)/shard_map/reduce_scatter | solution.py:286
  618.2 214.6 %reduce-scatter.35.cloned.1.call-start = ((), (), s32[]{:S(2)}) async-start(), calls=%async_computation.35 | async-start | bytes 1843200 | tf_op jit(solution)/shard_map/reduce_scatter | solution.py:275
  623.2 257.8 %reduce-scatter.23.cloned.1.call-start = ((), (), s32[]{:S(2)}) async-start(), calls=%async_computation.23 | async-start | bytes 1843200 | tf_op jit(solution)/shard_map/reduce_scatter | solution.py:275
  628.2 293.8 %reduce-scatter.27.cloned.1.call-start = ((), (), s32[]{:S(2)}) async-start(), calls=%async_computation.27 | async-start | bytes 1843200 | tf_op jit(solution)/shard_map/reduce_scatter | solution.py:275
  633.7 375.4 %reduce-scatter.57.cloned.1.call-start = ((), (), s32[]{:S(2)}) async-start(), calls=%async_computation.52 | async-start | bytes 2654208 | tf_op jit(solution)/shard_map/reduce_scatter | solution.py:346
  644.0 368.5 %reduce-scatter.59.cloned.1.call-start = ((), (), s32[]{:S(2)}) async-start(), calls=%async_computation.53 | async-start | bytes 2654208 | tf_op jit(solution)/shard_map/reduce_scatter | solution.py:347
  656.8 510.4 %reduce-scatter.55.cloned.1.call-start = ((), (), s32[]{:S(2)}) async-start(), calls=%async_computation.51 | async-start | bytes 663552 | tf_op jit(solution)/shard_map/reduce_scatter | solution.py:345
  789.9 137.3 %collective-permute-start.8 = (bf16[240,1,768]{2,0,1:T(8,128)(2,1)}, bf16[240,1,768]{2,0,1:T(8,128)(2,1)}, u32[]{:S(2)}, u32[]{:S(2)}) collective-permute-start(bf16[240,1,768]{2,0,1:T(8,128)(2,1)} %convert_element_type.831), channel_id=1, source_target_pairs={{0,3},{1,0},{2,1},{3,2},{4,7},{5,4},{6,5},{7,6},{8,11},{9,8},{10,9... | collective-permute-start | bytes 1105928 | tf_op jit(solution)/shard_map/ppermute | solution.py:304
  836.6 99.2 %collective-permute-start.11 = (bf16[240,1,768]{2,0,1:T(8,128)(2,1)}, bf16[240,1,768]{2,0,1:T(8,128)(2,1)}, u32[]{:S(2)}, u32[]{:S(2)}) collective-permute-start(bf16[240,1,768]{2,0,1:T(8,128)(2,1)} %convert_element_type.847), channel_id=1, source_target_pairs={{0,3},{1,0},{2,1},{3,2},{4,7},{5,4},{6,5},{7,6},{8,11},{9,8},{10,9... | collective-permute-start | bytes 1105928 | tf_op jit(solution)/shard_map/ppermute | solution.py:304
  1008.9 169.8 %all-gather.39.cloned.1.call-start = ((), (), s32[]{:S(2)}) async-start(), calls=%async_computation.48 | async-start | bytes 1327104 | tf_op jit(solution)/shard_map/all_gather | solution.py:361
  1010.7 170.9 %all-gather.41.cloned.1.call-start = ((), (), s32[]{:S(2)}) async-start(), calls=%async_computation.49 | async-start | bytes 1327104 | tf_op jit(solution)/shard_map/all_gather | solution.py:364
  1014.1 170.5 %reduce-scatter.53.cloned.1.call-start = ((), (), s32[]{:S(2)}) async-start(), calls=%async_computation.50 | async-start | bytes 2654208 | tf_op jit(solution)/shard_map/reduce_scatter | solution.py:344
  1136.3 111.0 %reduce-scatter.47.cloned.1.call-start = ((), (), s32[]{:S(2)}) async-start(), calls=%async_computation.44 | async-start | bytes 1843200 | tf_op jit(solution)/shard_map/reduce_scatter | solution.py:312
  1140.5 141.7 %reduce-scatter.43.cloned.1.call-start = ((), (), s32[]{:S(2)}) async-start(), calls=%async_computation.41 | async-start | bytes 1843200 | tf_op jit(solution)/shard_map/reduce_scatter | solution.py:312
  1144.4 173.4 %reduce-scatter.39.cloned.1.call-start = ((), (), s32[]{:S(2)}) async-start(), calls=%async_computation.38 | async-start | bytes 1843200 | tf_op jit(solution)/shard_map/reduce_scatter | solution.py:312
  (191 other events, 4424.0 us)
Sparse Core Ops, SparseCore 0:
  28.8 38.0 all-gather.14
  69.0 34.3 all-gather.18
  105.5 34.2 all-gather.22
  141.3 34.2 all-gather.26
  178.3 32.8 reduce-scatter.20
  214.0 32.6 reduce-scatter.24
  249.6 32.6 reduce-scatter.28
  284.6 32.6 reduce-scatter.32
  322.8 34.1 all-gather.28
  358.4 34.2 all-gather.36
  394.8 34.2 all-gather.24
  430.6 34.2 all-gather.34
  466.4 34.2 all-gather.20
  502.2 34.2 all-gather.32
  538.5 34.2 all-gather.16
  574.2 34.2 all-gather.30
  610.7 32.8 reduce-scatter.48
  646.4 32.6 reduce-scatter.44
  682.0 32.6 reduce-scatter.30
  716.9 32.6 reduce-scatter.40
  752.5 32.6 reduce-scatter.36
  787.5 45.1 reduce-scatter.34
  835.1 45.8 reduce-scatter.22
  883.2 38.7 reduce-scatter.26
  925.3 41.4 reduce-scatter.56
  970.1 42.3 reduce-scatter.58
  1016.0 34.3 reduce-scatter.54
  1132.7 43.3 reduce-scatter.52
  1178.4 33.8 reduce-scatter.50
  1214.6 32.6 reduce-scatter.46
  1249.5 32.6 reduce-scatter.42
  1285.1 32.6 reduce-scatter.38
  (2 shorter events, 47.7 us)
